TPU v7x, 32 devices: a whole 2x2x4 slice. The times are simulated.
32 devices in a mesh: group: 2 (over x), ctx: 16 (over z, y, core).
Axes of the slice: x: 2, y: 2, z: 4, core: 2. Of those that a mesh axis runs over, the one named last changes fastest.
Arguments:
- query_proj: bfloat16 [8192, 2048], P(('group', 'ctx')), parts along dimension 0, may hold values from -6 to 6
- key_proj: bfloat16 [8192, 2048], P(('group', 'ctx')), parts along dimension 0, may hold values from -6 to 6
- value_proj: bfloat16 [8192, 2048], P(('group', 'ctx')), parts along dimension 0, may hold values from -6 to 6
- short_weight: float32 [3, 3, 2048], replicated, may hold values from -3.5 to 3.5
- decay_rate: float32 [16, 2048], replicated, may hold values from 4.8828125e-05 to 0.125
- residue: float32 [16, 2048], replicated, may hold values from -0.5 to 0.5
- skip_gain: float32 [2048], replicated, may hold values from -4 to 4
Outputs:
- mixed: bfloat16 [8192, 2048], P(('group', 'ctx')), parts along dimension 0
There are 2 independent parts, one for each index of `group`. A program takes and returns all parts, laid end to end along the dimension named above; an argument that names none is the same for every part. Nothing has to cross between parts.
All inputs are finite; a program needn't handle non-finite values.
Results may differ from a plain program's by a relative error of at most 0.001.
Values may be sent and summed in bfloat16 or wider, within the bound.
A program may use at most 128 MiB of HBM per device.

v0:
```python
import functools

import jax
import jax.numpy as jnp
from jax import lax
from jax.experimental import pallas as pl
from jax.experimental.pallas import tpu as pltpu
from jax.sharding import PartitionSpec as P

MESH = pl.DeviceIdType.MESH
F32 = jnp.float32
BF16 = jnp.bfloat16
LANES = 128
SUBS = 8


def tree_sum(x):
    while x.shape[0] > 1:
        half = x.shape[0] // 2
        x = x[:half] + x[half:]
    return x[0]


def layer_kernel(
    parts, q_hbm, k_hbm, v_hbm, sw_hbm, rate_hbm, res_hbm, skip_hbm, out_hbm,
    qbuf, kbuf, vbuf, tail16, sw, rate, res, skip,
    perm, qx, kx, vx, tail, halo,
    a1, a32, a64, a128, a256, resp, g_s, y_s, x_s, w_s, z_s, qc_s,
    ends, got, back, inc, obuf,
    tail_sem, load_sem, par_sem, halo_sem, send_a, recv_a, send_b, recv_b, out_sem,
):
    tokens, channels = qbuf.shape
    modes = rate.shape[0]
    groups = channels // LANES
    steps = tokens // SUBS
    units = groups * modes // SUBS
    own = units // parts
    per_group = modes // SUBS // own
    me = lax.axis_index("ctx")
    barrier = pltpu.get_barrier_semaphore()

    tail_copies = []
    for i, src in enumerate((k_hbm, v_hbm, q_hbm)):
        c = pltpu.make_async_copy(src.at[pl.ds(tokens - 16, 16)], tail16.at[i], tail_sem.at[i])
        c.start()
        tail_copies.append(c)
    par_copies = []
    for i, (src, dst) in enumerate(((rate_hbm, rate), (res_hbm, res), (sw_hbm, sw), (skip_hbm, skip))):
        c = pltpu.make_async_copy(src, dst, par_sem.at[i])
        c.start()
        par_copies.append(c)
    loads = []
    for i, (src, dst) in enumerate(((k_hbm, kbuf), (v_hbm, vbuf), (q_hbm, qbuf))):
        c = pltpu.make_async_copy(src, dst, load_sem.at[i])
        c.start()
        loads.append(c)

    halo[...] = jnp.zeros(halo.shape, F32)

    def greet(i, carry):
        peer = lax.rem(me + i, parts)
        pl.semaphore_signal(barrier, inc=1, device_id={"ctx": peer}, device_id_type=MESH)
        return carry

    lax.fori_loop(1, parts, greet, 0)

    tail[...] = jnp.zeros(tail.shape, F32)
    for i in range(3):
        tail_copies[i].wait()
        tail[2 * i : 2 * i + 2, :] = tail16[i].astype(F32)[14:16, :]
    pl.semaphore_wait(barrier, parts - 1)

    halo_copy = pltpu.make_async_remote_copy(
        src_ref=tail, dst_ref=halo, send_sem=halo_sem.at[0], recv_sem=halo_sem.at[1],
        device_id={"ctx": lax.rem(me + 1, parts)}, device_id_type=MESH,
    )

    @pl.when(me < parts - 1)
    def _():
        halo_copy.start()

    for c in par_copies:
        c.wait()
    negative = -rate[...]
    a1[...] = jnp.exp(negative)
    a32[...] = jnp.exp(negative * steps)
    a64[...] = jnp.exp(negative * (2 * steps))
    a128[...] = jnp.exp(negative * (4 * steps))
    for u in range(units):
        col = (u * SUBS // modes) * LANES
        row = (u * SUBS) % modes
        a256[u] = jnp.exp(rate[row : row + SUBS, col : col + LANES] * (-float(tokens)))

    row_id = lax.broadcasted_iota(jnp.int32, (tokens, tokens), 0)
    col_id = lax.broadcasted_iota(jnp.int32, (tokens, tokens), 1)
    perm[0] = jnp.where(col_id == (row_id % SUBS) * steps + row_id // SUBS, 1.0, 0.0).astype(BF16)
    perm[1] = jnp.where(row_id == (col_id % SUBS) * steps + col_id // SUBS, 1.0, 0.0).astype(BF16)

    sub_f = lax.broadcasted_iota(jnp.int32, (SUBS, LANES), 0).astype(F32)
    sub_w = lax.broadcasted_iota(jnp.int32, (SUBS, channels), 0)
    sub_m = lax.broadcasted_iota(jnp.int32, (modes, SUBS, LANES), 1)

    def lanes_of(cg):
        return pl.ds(pl.multiple_of(cg * LANES, LANES), LANES)

    def spread(ref, lanes):
        return jnp.stack([jnp.broadcast_to(ref[n : n + 1, lanes], (SUBS, LANES)) for n in range(modes)])

    def response(cg, carry):
        lanes = lanes_of(cg)
        rates = spread(rate, lanes)
        wave = spread(res, lanes) * jnp.exp(rates * (-sub_f)[None])
        eight = jnp.exp(rates * (-float(SUBS)))
        for b in range(steps // SUBS):
            resp[cg, SUBS * b : SUBS * b + SUBS, :] = tree_sum(wave)
            if b + 1 < steps // SUBS:
                wave = wave * eight
        return carry

    lax.fori_loop(0, groups, response, 0)

    def permuted(buf, dst):
        for c in range(0, channels, 256):
            dst[2 * SUBS :, c : c + 256] = jnp.dot(
                perm[0], buf[:, c : c + 256], preferred_element_type=F32
            )

    def margin(dst, row):
        for lag in (1, 2):
            last = dst[2 * SUBS + tokens - SUBS * lag : 2 * SUBS + tokens - SUBS * (lag - 1), :]
            before = jnp.broadcast_to(halo[row + 2 - lag : row + 3 - lag, :], (SUBS, channels))
            dst[2 * SUBS - SUBS * lag : 2 * SUBS - SUBS * (lag - 1), :] = jnp.where(
                sub_w == 0, before, pltpu.roll(last, 1, 0)
            )

    loads[0].wait()
    permuted(kbuf, kx)
    loads[1].wait()
    permuted(vbuf, vx)

    @pl.when(me > 0)
    def _():
        halo_copy.wait_recv()

    margin(kx, 0)
    margin(vx, 2)

    def rows(j):
        return slice(SUBS * j, SUBS * j + SUBS)

    def tap(stream, lag, lanes):
        return jnp.broadcast_to(sw[stream, lag : lag + 1, lanes], (SUBS, LANES))

    def send_ends(owner):
        return pltpu.make_async_remote_copy(
            src_ref=ends.at[pl.ds(owner * own, own)], dst_ref=got.at[me],
            send_sem=send_a.at[owner], recv_sem=recv_a.at[me],
            device_id={"ctx": owner}, device_id_type=MESH,
        )

    def states(i, carry):
        cg = lax.rem(me * own // (modes // SUBS) + i, groups)
        lanes = lanes_of(cg)
        a = spread(a1, lanes)
        wk = [tap(1, lag, lanes) for lag in range(3)]
        wv = [tap(2, lag, lanes) for lag in range(3)]
        k2, k1 = kx[rows(0), lanes], kx[rows(1), lanes]
        v2, v1 = vx[rows(0), lanes], vx[rows(1), lanes]
        h = None
        for j in range(steps):
            k0, v0 = kx[rows(j + 2), lanes], vx[rows(j + 2), lanes]
            g = (wk[0] * k0 + wk[1] * k1 + wk[2] * k2) * (wv[0] * v0 + wv[1] * v1 + wv[2] * v2)
            k2, k1, v2, v1 = k1, k0, v1, v0
            g_s[cg, rows(j), :] = g
            h = jnp.broadcast_to(g[None], (modes, SUBS, LANES)) if h is None else a * h + g[None]
        for lag, ref in ((1, a32), (2, a64), (4, a128)):
            factor = jnp.where(sub_m >= lag, spread(ref, lanes), 0.0)
            h = h + factor * pltpu.roll(h, lag, 1)
        x_s[cg] = h
        for n in range(modes):
            ends[cg * (modes // SUBS) + n // SUBS, n % SUBS : n % SUBS + 1, :] = h[n, SUBS - 1 : SUBS, :]
        for p in range(per_group):
            owner = cg * per_group + p

            @pl.when(owner != me)
            def _():
                send_ends(owner).start()

            @pl.when(owner == me)
            def _():
                got[me] = ends[pl.ds(owner * own, own)]

        return carry

    lax.fori_loop(0, groups, states, 0)

    loads[2].wait()
    permuted(qbuf, qx)
    margin(qx, 4)

    def local(cg, carry):
        lanes = lanes_of(cg)
        gain = jnp.broadcast_to(skip[0:1, lanes], (SUBS, LANES))
        wq = [tap(0, lag, lanes) for lag in range(3)]
        for jb in range(steps // SUBS):
            acc = [None] * SUBS
            for ib in range(jb + 1):
                gs = [g_s[cg, rows(ib * SUBS + i), :] for i in range(SUBS)]
                base = SUBS * (jb - ib)
                taps = {
                    d: jnp.broadcast_to(resp[cg, base + d : base + d + 1, :], (SUBS, LANES))
                    for d in range(1 - SUBS, SUBS)
                    if base + d >= 0
                }
                for i in range(SUBS):
                    for j in range(SUBS):
                        if j - i in taps:
                            term = taps[j - i] * gs[i]
                            acc[j] = term if acc[j] is None else acc[j] + term
            for j in range(SUBS):
                at = jb * SUBS + j
                y_s[cg, rows(at), :] = acc[j] + gain * gs[j]
                qc_s[cg, rows(at), :] = (
                    wq[0] * qx[rows(at + 2), lanes]
                    + wq[1] * qx[rows(at + 1), lanes]
                    + wq[2] * qx[rows(at), lanes]
                )
        weights = spread(res, lanes)
        w_s[cg] = weights * jnp.exp(spread(rate, lanes) * (-(sub_f * steps + 1.0))[None])
        x = x_s[cg]
        x_s[cg] = jnp.where(sub_m >= 1, pltpu.roll(x, 1, 1), 0.0) * (weights * spread(a1, lanes))
        return carry

    def send_back(peer):
        return pltpu.make_async_remote_copy(
            src_ref=back.at[peer], dst_ref=inc.at[pl.ds(me * own, own)],
            send_sem=send_b.at[peer], recv_sem=recv_b.at[me],
            device_id={"ctx": peer}, device_id_type=MESH,
        )

    def arrive(owner):
        return pltpu.make_async_remote_copy(
            src_ref=back.at[owner], dst_ref=inc.at[pl.ds(owner * own, own)],
            send_sem=send_b.at[owner], recv_sem=recv_b.at[owner],
            device_id={"ctx": owner}, device_id_type=MESH,
        )

    lax.fori_loop(0, groups // 2, local, 0)

    def took(p, total):
        @pl.when(p != me)
        def _():
            pltpu.make_async_remote_copy(
                src_ref=ends.at[pl.ds(p * own, own)], dst_ref=got.at[p],
                send_sem=send_a.at[p], recv_sem=recv_a.at[p],
                device_id={"ctx": p}, device_id_type=MESH,
            ).wait_recv()

        back[p] = total

        @pl.when(p != me)
        def _():
            send_back(p).start()

        @pl.when(p == me)
        def _():
            inc[pl.ds(me * own, own)] = total

        return a256[pl.ds(me * own, own)] * total + got[p]

    lax.fori_loop(0, parts, took, jnp.zeros((own, SUBS, LANES), F32))

    lax.fori_loop(groups // 2, groups, local, 0)

    def finish(cg, carry):
        lanes = lanes_of(cg)
        for p in range(per_group):
            owner = cg * per_group + p

            @pl.when(owner != me)
            def _():
                arrive(owner).wait_recv()

        first = cg * (modes // SUBS)
        entry = jnp.stack(
            [
                jnp.broadcast_to(inc[first + n // SUBS, n % SUBS : n % SUBS + 1, :], (SUBS, LANES))
                for n in range(modes)
            ]
        )
        a = spread(a1, lanes)
        h = w_s[cg] * entry + x_s[cg]
        for j in range(0, steps, 2):
            pair = []
            for i in (j, j + 1):
                pair.append(qc_s[cg, rows(i), :] * (y_s[cg, rows(i), :] + tree_sum(h)))
                if i + 1 < steps:
                    h = a * h
            z_s[SUBS * j : SUBS * (j + 2), lanes] = jnp.concatenate(pair, axis=0).astype(BF16)
        return carry

    outs = []
    pieces = 4
    for s in range(pieces):
        lax.fori_loop(s * groups // pieces, (s + 1) * groups // pieces, finish, 0)
        width = channels // pieces
        for c in range(s * width, (s + 1) * width, 256):
            obuf[:, c : c + 256] = jnp.dot(
                perm[1], z_s[:, c : c + 256], preferred_element_type=F32
            ).astype(BF16)
        cols = pl.ds(s * width, width)
        c = pltpu.make_async_copy(obuf.at[:, cols], out_hbm.at[:, cols], out_sem.at[s])
        c.start()
        outs.append(c)

    @pl.when(me < parts - 1)
    def _():
        halo_copy.wait_send()

    def sent(p, carry):
        @pl.when(p != me)
        def _():
            send_ends(p).wait_send()
            send_back(p).wait_send()

        return carry

    lax.fori_loop(0, parts, sent, 0)
    for c in outs:
        c.wait()


def per_device(query_proj, key_proj, value_proj, short_weight, decay_rate, residue, skip_gain):
    parts = lax.axis_size("ctx")
    tokens, channels = query_proj.shape
    modes = decay_rate.shape[0]
    groups = channels // LANES
    steps = tokens // SUBS
    units = groups * modes // SUBS
    own = units // parts
    any_space = pl.BlockSpec(memory_space=pl.ANY)
    vm = pltpu.VMEM
    dma = pltpu.SemaphoreType.DMA
    return pl.pallas_call(
        functools.partial(layer_kernel, parts),
        out_shape=jax.ShapeDtypeStruct((tokens, channels), BF16),
        in_specs=[any_space] * 7,
        out_specs=any_space,
        scratch_shapes=[
            vm((tokens, channels), BF16),
            vm((tokens, channels), BF16),
            vm((tokens, channels), BF16),
            vm((3, 16, channels), BF16),
            vm(short_weight.shape, F32),
            vm(decay_rate.shape, F32),
            vm(residue.shape, F32),
            vm((1, channels), F32),
            vm((2, tokens, tokens), BF16),
            vm((tokens + 2 * SUBS, channels), F32),
            vm((tokens + 2 * SUBS, channels), F32),
            vm((tokens + 2 * SUBS, channels), F32),
            vm((SUBS, channels), F32),
            vm((SUBS, channels), F32),
            vm((modes, channels), F32),
            vm((modes, channels), F32),
            vm((modes, channels), F32),
            vm((modes, channels), F32),
            vm((units, SUBS, LANES), F32),
            vm((groups, steps, LANES), F32),
            vm((groups, tokens, LANES), F32),
            vm((groups, tokens, LANES), F32),
            vm((groups, modes, SUBS, LANES), F32),
            vm((groups, modes, SUBS, LANES), F32),
            vm((tokens, channels), BF16),
            vm((groups, tokens, LANES), F32),
            vm((units, SUBS, LANES), F32),
            vm((parts, own, SUBS, LANES), F32),
            vm((parts, own, SUBS, LANES), F32),
            vm((units, SUBS, LANES), F32),
            vm((tokens, channels), BF16),
            dma((3,)),
            dma((3,)),
            dma((4,)),
            dma((2,)),
            dma((parts,)),
            dma((parts,)),
            dma((parts,)),
            dma((parts,)),
            dma((4,)),
        ],
        compiler_params=pltpu.CompilerParams(
            collective_id=0, has_side_effects=True, vmem_limit_bytes=48 * 1024 * 1024
        ),
    )(
        query_proj, key_proj, value_proj, short_weight, decay_rate, residue,
        skip_gain.reshape(1, channels),
    )


def solution(mesh):
    rows = P(("group", "ctx"), None)
    return jax.shard_map(
        per_device,
        mesh=mesh,
        in_specs=(rows, rows, rows, P(), P(), P(), P()),
        out_specs=rows,
        check_vma=False,
    )
```

profile of v0, /device:TPU:25, one launch (start us, length us, event | category | flops | bytes accessed | tf_op | source)
XLA Modules:
  0.0 30.8 jit_solution(2576469682310877467)
XLA Ops:
  0.0 0.0 copy-start
  0.0 1.2 %copy-done = bf16[256,2048]{1,0:T(8,128)(2,1)S(1)} copy-done((bf16[256,2048]{1,0:T(8,128)(2,1)S(1)}, bf16[256,2048]{1,0:T(8,128)(2,1)}, u32[]{:S(2)}) %copy-start) | copy-done | bytes 1048600
  1.2 0.0 copy-start.1
  1.2 1.2 %copy-done.1 = bf16[256,2048]{1,0:T(8,128)(2,1)S(1)} copy-done((bf16[256,2048]{1,0:T(8,128)(2,1)S(1)}, bf16[256,2048]{1,0:T(8,128)(2,1)}, u32[]{:S(2)}) %copy-start.1) | copy-done | bytes 1048600
  2.5 0.0 copy-start.2
  2.5 1.2 %copy-done.2 = bf16[256,2048]{1,0:T(8,128)(2,1)S(1)} copy-done((bf16[256,2048]{1,0:T(8,128)(2,1)S(1)}, bf16[256,2048]{1,0:T(8,128)(2,1)}, u32[]{:S(2)}) %copy-start.2) | copy-done | bytes 1048600
  3.7 0.0 copy-start.3
  3.7 0.9 %copy-done.3 = f32[16,2048]{1,0:T(8,128)S(1)} copy-done((f32[16,2048]{1,0:T(8,128)S(1)}, f32[16,2048]{1,0:T(8,128)}, u32[]{:S(2)}) %copy-start.3) | copy-done | bytes 131096
  4.6 0.0 copy-start.4
  4.6 0.9 %copy-done.4 = f32[16,2048]{1,0:T(8,128)S(1)} copy-done((f32[16,2048]{1,0:T(8,128)S(1)}, f32[16,2048]{1,0:T(8,128)}, u32[]{:S(2)}) %copy-start.4) | copy-done | bytes 131096
  5.5 0.0 copy-start.5
  5.5 0.9 %copy-done.5 = f32[3,3,2048]{2,1,0:T(4,128)S(1)} copy-done((f32[3,3,2048]{2,1,0:T(4,128)S(1)}, f32[3,3,2048]{2,1,0:T(4,128)}, u32[]{:S(2)}) %copy-start.5) | copy-done | bytes 73752
  6.4 0.0 copy-start.6
  6.4 0.7 %copy-done.6 = f32[2048]{0:T(1024)S(1)} copy-done((f32[2048]{0:T(1024)S(1)}, f32[2048]{0:T(1024)}, u32[]{:S(2)}) %copy-start.6) | copy-done | bytes 8216
  7.1 22.7 %shard_map.73 = bf16[256,2048]{1,0:T(8,128)(2,1)S(1)} custom-call(bf16[256,2048]{1,0:T(8,128)(2,1)S(1)} %copy-done, bf16[256,2048]{1,0:T(8,128)(2,1)S(1)} %copy-done.1, bf16[256,2048]{1,0:T(8,128)(2,1)S(1)} %copy-done.2, f32[3,3,2048]{2,1,0:T(4,128)S(1)} %copy-done.5, f32[16,2048]{1,0:T(8,128)S(1)} %copy-done.3, f32[16,2048]{1,0:T(8,128)S(1)} %copy-done.4, ...), custom_call_target="tpu_custom_call" | custom-call | tf_op jit(solution)/shard_map/pallas_call | solution.py:344
  29.8 1.0 %copy.9 = bf16[256,2048]{1,0:T(8,128)(2,1)} copy(bf16[256,2048]{1,0:T(8,128)(2,1)S(1)} %shard_map.73) | data formatting | bytes 2097152
Async XLA Ops:
  0.0 1.2 %copy-start = (bf16[256,2048]{1,0:T(8,128)(2,1)S(1)}, bf16[256,2048]{1,0:T(8,128)(2,1)}, u32[]{:S(2)}) copy-start(bf16[256,2048]{1,0:T(8,128)(2,1)} %q_hbm.1) | copy-start | bytes 3145732
  1.2 1.2 %copy-start.1 = (bf16[256,2048]{1,0:T(8,128)(2,1)S(1)}, bf16[256,2048]{1,0:T(8,128)(2,1)}, u32[]{:S(2)}) copy-start(bf16[256,2048]{1,0:T(8,128)(2,1)} %k_hbm.1) | copy-start | bytes 3145732
  2.5 1.2 %copy-start.2 = (bf16[256,2048]{1,0:T(8,128)(2,1)S(1)}, bf16[256,2048]{1,0:T(8,128)(2,1)}, u32[]{:S(2)}) copy-start(bf16[256,2048]{1,0:T(8,128)(2,1)} %v_hbm.1) | copy-start | bytes 3145732
  3.7 0.9 %copy-start.3 = (f32[16,2048]{1,0:T(8,128)S(1)}, f32[16,2048]{1,0:T(8,128)}, u32[]{:S(2)}) copy-start(f32[16,2048]{1,0:T(8,128)} %rate_hbm.1) | copy-start | bytes 393220
  4.6 0.9 %copy-start.4 = (f32[16,2048]{1,0:T(8,128)S(1)}, f32[16,2048]{1,0:T(8,128)}, u32[]{:S(2)}) copy-start(f32[16,2048]{1,0:T(8,128)} %res_hbm.1) | copy-start | bytes 393220
  5.5 0.9 %copy-start.5 = (f32[3,3,2048]{2,1,0:T(4,128)S(1)}, f32[3,3,2048]{2,1,0:T(4,128)}, u32[]{:S(2)}) copy-start(f32[3,3,2048]{2,1,0:T(4,128)} %sw_hbm.1) | copy-start | bytes 221188
  6.4 0.7 %copy-start.6 = (f32[2048]{0:T(1024)S(1)}, f32[2048]{0:T(1024)}, u32[]{:S(2)}) copy-start(f32[2048]{0:T(1024)} %param.13) | copy-start | bytes 24580
where the time goes:
time: 31.1 us; the launch traced here: 30.8 us
  Pallas kernels  22.7 us (73%)
  local copies, waits for them, and re-layouts  8.04 us (26%)
    pallas_call x1, Pallas kernels, per_device(): pl.pallas_call(functools.partial(layer_kernel, parts), out_shape=jax.Shap...  22.7 us
    unnamed x15, local copies, waits for them, and re-layouts  8.04 us

commit v1 on v0

--- a/solution.py
+++ b/solution.py
@@ -23,11 +23,11 @@
 
 def layer_kernel(
     parts, q_hbm, k_hbm, v_hbm, sw_hbm, rate_hbm, res_hbm, skip_hbm, out_hbm,
-    qbuf, kbuf, vbuf, tail16, sw, rate, res, skip,
+    qbuf, kbuf, vbuf, sw, rate, res, skip,
     perm, qx, kx, vx, tail, halo,
-    a1, a32, a64, a128, a256, resp, g_s, y_s, x_s, w_s, z_s, qc_s,
+    a1, a32, a64, a128, a256, inv1, inv2, resp, g_s, y_s, x_s, w_s, z_s, qc_s,
     ends, got, back, inc, obuf,
-    tail_sem, load_sem, par_sem, halo_sem, send_a, recv_a, send_b, recv_b, out_sem,
+    load_sem, par_sem, halo_sem, send_a, recv_a, send_b, recv_b, out_sem,
 ):
     tokens, channels = qbuf.shape
     modes = rate.shape[0]
@@ -39,11 +39,6 @@
     me = lax.axis_index("ctx")
     barrier = pltpu.get_barrier_semaphore()
 
-    tail_copies = []
-    for i, src in enumerate((k_hbm, v_hbm, q_hbm)):
-        c = pltpu.make_async_copy(src.at[pl.ds(tokens - 16, 16)], tail16.at[i], tail_sem.at[i])
-        c.start()
-        tail_copies.append(c)
     par_copies = []
     for i, (src, dst) in enumerate(((rate_hbm, rate), (res_hbm, res), (sw_hbm, sw), (skip_hbm, skip))):
         c = pltpu.make_async_copy(src, dst, par_sem.at[i])
@@ -64,21 +59,6 @@
 
     lax.fori_loop(1, parts, greet, 0)
 
-    tail[...] = jnp.zeros(tail.shape, F32)
-    for i in range(3):
-        tail_copies[i].wait()
-        tail[2 * i : 2 * i + 2, :] = tail16[i].astype(F32)[14:16, :]
-    pl.semaphore_wait(barrier, parts - 1)
-
-    halo_copy = pltpu.make_async_remote_copy(
-        src_ref=tail, dst_ref=halo, send_sem=halo_sem.at[0], recv_sem=halo_sem.at[1],
-        device_id={"ctx": lax.rem(me + 1, parts)}, device_id_type=MESH,
-    )
-
-    @pl.when(me < parts - 1)
-    def _():
-        halo_copy.start()
-
     for c in par_copies:
         c.wait()
     negative = -rate[...]
@@ -89,7 +69,10 @@
     for u in range(units):
         col = (u * SUBS // modes) * LANES
         row = (u * SUBS) % modes
-        a256[u] = jnp.exp(rate[row : row + SUBS, col : col + LANES] * (-float(tokens)))
+        part = rate[row : row + SUBS, col : col + LANES]
+        a256[u] = jnp.exp(part * (-float(tokens)))
+        inv1[u] = jnp.exp(part)
+        inv2[u] = jnp.exp(part * 2.0)
 
     row_id = lax.broadcasted_iota(jnp.int32, (tokens, tokens), 0)
     col_id = lax.broadcasted_iota(jnp.int32, (tokens, tokens), 1)
@@ -125,25 +108,24 @@
                 perm[0], buf[:, c : c + 256], preferred_element_type=F32
             )
 
-    def margin(dst, row):
+    def margin(dst):
         for lag in (1, 2):
             last = dst[2 * SUBS + tokens - SUBS * lag : 2 * SUBS + tokens - SUBS * (lag - 1), :]
-            before = jnp.broadcast_to(halo[row + 2 - lag : row + 3 - lag, :], (SUBS, channels))
             dst[2 * SUBS - SUBS * lag : 2 * SUBS - SUBS * (lag - 1), :] = jnp.where(
-                sub_w == 0, before, pltpu.roll(last, 1, 0)
+                sub_w == 0, 0.0, pltpu.roll(last, 1, 0)
             )
 
-    loads[0].wait()
-    permuted(kbuf, kx)
-    loads[1].wait()
-    permuted(vbuf, vx)
-
-    @pl.when(me > 0)
-    def _():
-        halo_copy.wait_recv()
-
-    margin(kx, 0)
-    margin(vx, 2)
+    last_rows = [2 * SUBS + SUBS * (steps - lag) + SUBS - 1 for lag in (2, 1)]
+    head_rows = [2 * SUBS, 3 * SUBS]
+
+    for c, buf, dst in zip(loads, (kbuf, vbuf, qbuf), (kx, vx, qx)):
+        c.wait()
+        permuted(buf, dst)
+        margin(dst)
+    tail[...] = jnp.zeros(tail.shape, F32)
+    for i, src in enumerate((kx, vx, qx)):
+        for b, r in enumerate(last_rows):
+            tail[2 * i + b : 2 * i + b + 1, :] = src[r : r + 1, :]
 
     def rows(j):
         return slice(SUBS * j, SUBS * j + SUBS)
@@ -153,13 +135,23 @@
 
     def send_ends(owner):
         return pltpu.make_async_remote_copy(
-            src_ref=ends.at[pl.ds(owner * own, own)], dst_ref=got.at[me],
+            src_ref=ends.at[owner], dst_ref=got.at[me],
             send_sem=send_a.at[owner], recv_sem=recv_a.at[me],
             device_id={"ctx": owner}, device_id_type=MESH,
         )
 
-    def states(i, carry):
-        cg = lax.rem(me * own // (modes // SUBS) + i, groups)
+    def gated_change(w, tails, heads):
+        own_row, full = [], []
+        for m in range(2):
+            w0, w1, w2 = w[3 * m], w[3 * m + 1], w[3 * m + 2]
+            before2, before1 = tails[2 * m], tails[2 * m + 1]
+            x0, x1 = heads[2 * m], heads[2 * m + 1]
+            zero = (w0 * x0, w0 * x1 + w1 * x0)
+            own_row.append(zero)
+            full.append((zero[0] + w1 * before1 + w2 * before2, zero[1] + w2 * before1))
+        return [full[0][t] * full[1][t] - own_row[0][t] * own_row[1][t] for t in range(2)]
+
+    def states(cg, carry):
         lanes = lanes_of(cg)
         a = spread(a1, lanes)
         wk = [tap(1, lag, lanes) for lag in range(3)]
@@ -177,26 +169,37 @@
             factor = jnp.where(sub_m >= lag, spread(ref, lanes), 0.0)
             h = h + factor * pltpu.roll(h, lag, 1)
         x_s[cg] = h
-        for n in range(modes):
-            ends[cg * (modes // SUBS) + n // SUBS, n % SUBS : n % SUBS + 1, :] = h[n, SUBS - 1 : SUBS, :]
         for p in range(per_group):
             owner = cg * per_group + p
-
-            @pl.when(owner != me)
-            def _():
-                send_ends(owner).start()
-
-            @pl.when(owner == me)
-            def _():
-                got[me] = ends[pl.ds(owner * own, own)]
-
+            for n in range(own * SUBS):
+                m = p * own * SUBS + n
+                ends[owner, n // SUBS, n % SUBS : n % SUBS + 1, :] = h[m, SUBS - 1 : SUBS, :]
+            line = 0
+            for spots in (last_rows, head_rows):
+                for src in (kx, vx):
+                    for r in spots:
+                        ends[owner, own, line : line + 1, :] = src[r : r + 1, lanes]
+                        line += 1
         return carry
 
     lax.fori_loop(0, groups, states, 0)
 
-    loads[2].wait()
-    permuted(qbuf, qx)
-    margin(qx, 4)
+    pl.semaphore_wait(barrier, parts - 1)
+    halo_copy = pltpu.make_async_remote_copy(
+        src_ref=tail, dst_ref=halo, send_sem=halo_sem.at[0], recv_sem=halo_sem.at[1],
+        device_id={"ctx": lax.rem(me + 1, parts)}, device_id_type=MESH,
+    )
+
+    def send_all(i, carry):
+        send_ends(lax.rem(me + i, parts)).start()
+        return carry
+
+    lax.fori_loop(1, parts, send_all, 0)
+    got[me] = ends[me]
+
+    @pl.when(me < parts - 1)
+    def _():
+        halo_copy.start()
 
     def local(cg, carry):
         lanes = lanes_of(cg)
@@ -245,17 +248,28 @@
             device_id={"ctx": owner}, device_id_type=MESH,
         )
 
-    lax.fori_loop(0, groups // 2, local, 0)
-
-    def took(p, total):
+    lax.fori_loop(0, groups * 3 // 4, local, 0)
+
+    mine = pl.ds(me * own, own)
+    own_lanes = lanes_of(me * own // (modes // SUBS))
+    own_w = [sw[m, lag : lag + 1, own_lanes] for m in (1, 2) for lag in range(3)]
+
+    def took(p, carry):
+        total, before = carry
+
         @pl.when(p != me)
         def _():
             pltpu.make_async_remote_copy(
-                src_ref=ends.at[pl.ds(p * own, own)], dst_ref=got.at[p],
+                src_ref=ends.at[p], dst_ref=got.at[p],
                 send_sem=send_a.at[p], recv_sem=recv_a.at[p],
                 device_id={"ctx": p}, device_id_type=MESH,
             ).wait_recv()
 
+        extra = got[p, own]
+        tails = [before[i : i + 1, :] for i in range(4)]
+        heads = [extra[i : i + 1, :] for i in range(4, 8)]
+        d0, d1 = gated_change(own_w, tails, heads)
+        total = total + (inv1[mine] * d0[None] + inv2[mine] * d1[None])
         back[p] = total
 
         @pl.when(p != me)
@@ -264,13 +278,36 @@
 
         @pl.when(p == me)
         def _():
-            inc[pl.ds(me * own, own)] = total
-
-        return a256[pl.ds(me * own, own)] * total + got[p]
-
-    lax.fori_loop(0, parts, took, jnp.zeros((own, SUBS, LANES), F32))
-
-    lax.fori_loop(groups // 2, groups, local, 0)
+            inc[mine] = total
+
+        return a256[mine] * total + got[p, 0:own], extra
+
+    lax.fori_loop(
+        0, parts, took,
+        (jnp.zeros((own, SUBS, LANES), F32), jnp.zeros((SUBS, LANES), F32)),
+    )
+
+    lax.fori_loop(groups * 3 // 4, groups, local, 0)
+
+    @pl.when(me > 0)
+    def _():
+        halo_copy.wait_recv()
+
+    def repair(cg, carry):
+        lanes = lanes_of(cg)
+        tails = [halo[i : i + 1, lanes] for i in range(6)]
+        heads = [src[r : r + 1, lanes] for src in (kx, vx) for r in head_rows]
+        w = [sw[m, lag : lag + 1, lanes] for m in (1, 2, 0) for lag in range(3)]
+        d0, d1 = gated_change(w, tails, heads)
+        gain = skip[0:1, lanes]
+        early = jnp.sum(res[:, lanes] * jnp.exp(rate[:, lanes]), axis=0, keepdims=True)
+        y_s[cg, 0:1, :] = y_s[cg, 0:1, :] + (gain * d0 - early * d1)
+        y_s[cg, SUBS : SUBS + 1, :] = y_s[cg, SUBS : SUBS + 1, :] + gain * d1
+        qc_s[cg, 0:1, :] = qc_s[cg, 0:1, :] + (w[7] * tails[5] + w[8] * tails[4])
+        qc_s[cg, SUBS : SUBS + 1, :] = qc_s[cg, SUBS : SUBS + 1, :] + w[8] * tails[5]
+        return carry
+
+    lax.fori_loop(0, groups, repair, 0)
 
     def finish(cg, carry):
         lanes = lanes_of(cg)
@@ -338,7 +375,7 @@
     steps = tokens // SUBS
     units = groups * modes // SUBS
     own = units // parts
-    any_space = pl.BlockSpec(memory_space=pl.ANY)
+    any_space = pl.BlockSpec(memory_space=pltpu.HBM)
     vm = pltpu.VMEM
     dma = pltpu.SemaphoreType.DMA
     return pl.pallas_call(
@@ -350,7 +387,6 @@
             vm((tokens, channels), BF16),
             vm((tokens, channels), BF16),
             vm((tokens, channels), BF16),
-            vm((3, 16, channels), BF16),
             vm(short_weight.shape, F32),
             vm(decay_rate.shape, F32),
             vm(residue.shape, F32),
@@ -366,6 +402,8 @@
             vm((modes, channels), F32),
             vm((modes, channels), F32),
             vm((units, SUBS, LANES), F32),
+            vm((units, SUBS, LANES), F32),
+            vm((units, SUBS, LANES), F32),
             vm((groups, steps, LANES), F32),
             vm((groups, tokens, LANES), F32),
             vm((groups, tokens, LANES), F32),
@@ -373,12 +411,11 @@
             vm((groups, modes, SUBS, LANES), F32),
             vm((tokens, channels), BF16),
             vm((groups, tokens, LANES), F32),
-            vm((units, SUBS, LANES), F32),
-            vm((parts, own, SUBS, LANES), F32),
+            vm((parts, own + 1, SUBS, LANES), F32),
+            vm((parts, own + 1, SUBS, LANES), F32),
             vm((parts, own, SUBS, LANES), F32),
             vm((units, SUBS, LANES), F32),
             vm((tokens, channels), BF16),
-            dma((3,)),
             dma((3,)),
             dma((4,)),
             dma((2,)),
@@ -389,7 +426,7 @@
             dma((4,)),
         ],
         compiler_params=pltpu.CompilerParams(
-            collective_id=0, has_side_effects=True, vmem_limit_bytes=48 * 1024 * 1024
+            collective_id=0, has_side_effects=True, vmem_limit_bytes=63 * 1024 * 1024
         ),
     )(
         query_proj, key_proj, value_proj, short_weight, decay_rate, residue,

time: 31.1 us -> 24.9 us (0.80)
  local copies, waits for them, and re-layouts: 8.04 us -> 2.3 us
    unnamed x15 -> x1, local copies, waits for them, and re-layouts: 8.04 us -> 2.3 us
where the time goes in v1:
time: 24.9 us; the launch traced here: 24.8 us
  Pallas kernels  22.4 us (90%)
  local copies, waits for them, and re-layouts  2.3 us (9%)
    pallas_call x1, Pallas kernels, per_device(): pl.pallas_call(functools.partial(layer_kernel, parts), out_shape=jax.Shap...  22.4 us
    unnamed x1, local copies, waits for them, and re-layouts  2.3 us

profile of v1, /device:TPU:25, one launch (start us, length us, event | category | flops | bytes accessed | tf_op | source)
XLA Modules:
  0.0 24.8 jit_solution(14628902864243562044)
XLA Ops:
  0.0 22.4 %shard_map.73 = bf16[256,2048]{1,0:T(8,128)(2,1)} custom-call(bf16[256,2048]{1,0:T(8,128)(2,1)} %q_hbm.1, bf16[256,2048]{1,0:T(8,128)(2,1)} %k_hbm.1, bf16[256,2048]{1,0:T(8,128)(2,1)} %v_hbm.1, f32[3,3,2048]{2,1,0:T(4,128)} %sw_hbm.1, f32[16,2048]{1,0:T(8,128)} %rate_hbm.1, f32[16,2048]{1,0:T(8,128)} %res_hbm.1, f32[1,2048]{1,0:T(1,128)} %bitcast.1), custom_call_target="tpu_custom_call" | custom-call | tf_op jit(solution)/shard_map/pallas_call | solution.py:381
  22.5 2.3 %copy.9 = bf16[256,2048]{1,0:T(8,128)(2,1)} copy(bf16[256,2048]{1,0:T(8,128)(2,1)} %shard_map.73) | data formatting | bytes 2097152

commit v2 on v1

--- a/solution.py
+++ b/solution.py
@@ -22,12 +22,12 @@
 
 
 def layer_kernel(
-    parts, q_hbm, k_hbm, v_hbm, sw_hbm, rate_hbm, res_hbm, skip_hbm, out_hbm,
+    parts, q_hbm, k_hbm, v_hbm, sw_hbm, rate_hbm, res_hbm, skip_hbm, out_ref,
     qbuf, kbuf, vbuf, sw, rate, res, skip,
     perm, qx, kx, vx, tail, halo,
-    a1, a32, a64, a128, a256, inv1, inv2, resp, g_s, y_s, x_s, w_s, z_s, qc_s,
-    ends, got, back, inc, obuf,
-    load_sem, par_sem, halo_sem, send_a, recv_a, send_b, recv_b, out_sem,
+    a1, a32, a64, a128, a256, inv1, inv2, resp, g_s, y_s, x_s, w_s, qc_s,
+    ends, got, back, inc,
+    load_sem, par_sem, halo_sem, send_a, recv_a, send_b, recv_b,
 ):
     tokens, channels = qbuf.shape
     modes = rate.shape[0]
@@ -76,8 +76,7 @@
 
     row_id = lax.broadcasted_iota(jnp.int32, (tokens, tokens), 0)
     col_id = lax.broadcasted_iota(jnp.int32, (tokens, tokens), 1)
-    perm[0] = jnp.where(col_id == (row_id % SUBS) * steps + row_id // SUBS, 1.0, 0.0).astype(BF16)
-    perm[1] = jnp.where(row_id == (col_id % SUBS) * steps + col_id // SUBS, 1.0, 0.0).astype(BF16)
+    perm[...] = jnp.where(col_id == (row_id % SUBS) * steps + row_id // SUBS, 1.0, 0.0).astype(BF16)
 
     sub_f = lax.broadcasted_iota(jnp.int32, (SUBS, LANES), 0).astype(F32)
     sub_w = lax.broadcasted_iota(jnp.int32, (SUBS, channels), 0)
@@ -105,7 +104,7 @@
     def permuted(buf, dst):
         for c in range(0, channels, 256):
             dst[2 * SUBS :, c : c + 256] = jnp.dot(
-                perm[0], buf[:, c : c + 256], preferred_element_type=F32
+                perm[...], buf[:, c : c + 256], preferred_element_type=F32
             )
 
     def margin(dst):
@@ -327,28 +326,16 @@
         )
         a = spread(a1, lanes)
         h = w_s[cg] * entry + x_s[cg]
-        for j in range(0, steps, 2):
-            pair = []
-            for i in (j, j + 1):
-                pair.append(qc_s[cg, rows(i), :] * (y_s[cg, rows(i), :] + tree_sum(h)))
-                if i + 1 < steps:
-                    h = a * h
-            z_s[SUBS * j : SUBS * (j + 2), lanes] = jnp.concatenate(pair, axis=0).astype(BF16)
-        return carry
-
-    outs = []
-    pieces = 4
-    for s in range(pieces):
-        lax.fori_loop(s * groups // pieces, (s + 1) * groups // pieces, finish, 0)
-        width = channels // pieces
-        for c in range(s * width, (s + 1) * width, 256):
-            obuf[:, c : c + 256] = jnp.dot(
-                perm[1], z_s[:, c : c + 256], preferred_element_type=F32
-            ).astype(BF16)
-        cols = pl.ds(s * width, width)
-        c = pltpu.make_async_copy(obuf.at[:, cols], out_hbm.at[:, cols], out_sem.at[s])
-        c.start()
-        outs.append(c)
+        for j in range(steps):
+            g_s[cg, pl.ds(j, SUBS, stride=steps), :] = qc_s[cg, rows(j), :] * (
+                y_s[cg, rows(j), :] + tree_sum(h)
+            )
+            if j + 1 < steps:
+                h = a * h
+        out_ref[:, lanes] = g_s[cg].astype(BF16)
+        return carry
+
+    lax.fori_loop(0, groups, finish, 0)
 
     @pl.when(me < parts - 1)
     def _():
@@ -363,8 +350,6 @@
         return carry
 
     lax.fori_loop(0, parts, sent, 0)
-    for c in outs:
-        c.wait()
 
 
 def per_device(query_proj, key_proj, value_proj, short_weight, decay_rate, residue, skip_gain):
@@ -380,9 +365,9 @@
     dma = pltpu.SemaphoreType.DMA
     return pl.pallas_call(
         functools.partial(layer_kernel, parts),
-        out_shape=jax.ShapeDtypeStruct((tokens, channels), BF16),
+        out_shape=pltpu.VMEM((tokens, channels), BF16),
         in_specs=[any_space] * 7,
-        out_specs=any_space,
+        out_specs=pl.BlockSpec(memory_space=pltpu.VMEM),
         scratch_shapes=[
             vm((tokens, channels), BF16),
             vm((tokens, channels), BF16),
@@ -391,7 +376,7 @@
             vm(decay_rate.shape, F32),
             vm(residue.shape, F32),
             vm((1, channels), F32),
-            vm((2, tokens, tokens), BF16),
+            vm((tokens, tokens), BF16),
             vm((tokens + 2 * SUBS, channels), F32),
             vm((tokens + 2 * SUBS, channels), F32),
             vm((tokens + 2 * SUBS, channels), F32),
@@ -409,13 +394,11 @@
             vm((groups, tokens, LANES), F32),
             vm((groups, modes, SUBS, LANES), F32),
             vm((groups, modes, SUBS, LANES), F32),
-            vm((tokens, channels), BF16),
             vm((groups, tokens, LANES), F32),
             vm((parts, own + 1, SUBS, LANES), F32),
             vm((parts, own + 1, SUBS, LANES), F32),
             vm((parts, own, SUBS, LANES), F32),
             vm((units, SUBS, LANES), F32),
-            vm((tokens, channels), BF16),
             dma((3,)),
             dma((4,)),
             dma((2,)),
@@ -423,10 +406,9 @@
             dma((parts,)),
             dma((parts,)),
             dma((parts,)),
-            dma((4,)),
         ],
         compiler_params=pltpu.CompilerParams(
-            collective_id=0, has_side_effects=True, vmem_limit_bytes=63 * 1024 * 1024
+            collective_id=0, has_side_effects=True, vmem_limit_bytes=62 * 1024 * 1024
         ),
     )(
         query_proj, key_proj, value_proj, short_weight, decay_rate, residue,

time: 24.9 us -> 22.5 us (0.904)
  local copies, waits for them, and re-layouts: 2.3 us -> 0.97 us
  Pallas kernels: 22.4 us -> 21.4 us
    unnamed x1, local copies, waits for them, and re-layouts: 2.3 us -> 0.97 us
    pallas_call x1, Pallas kernels: 22.4 us -> 21.4 us  [per_device(): pl.pallas_call(functools.partial(layer_kernel, parts), out_shape=pltpu.VM...]
where the time goes in v2:
time: 22.5 us; the launch traced here: 22.4 us
  Pallas kernels  21.4 us (95%)
  local copies, waits for them, and re-layouts  0.97 us (4%)
    pallas_call x1, Pallas kernels, per_device(): pl.pallas_call(functools.partial(layer_kernel, parts), out_shape=pltpu.VM...  21.4 us
    unnamed x1, local copies, waits for them, and re-layouts  0.97 us

profile of v2, /device:TPU:25, one launch (start us, length us, event | category | flops | bytes accessed | tf_op | source)
XLA Modules:
  0.0 22.4 jit_solution(17528210027613319469)
XLA Ops:
  0.0 21.4 %shard_map.73 = bf16[256,2048]{1,0:T(8,128)(2,1)S(1)} custom-call(bf16[256,2048]{1,0:T(8,128)(2,1)} %q_hbm.1, bf16[256,2048]{1,0:T(8,128)(2,1)} %k_hbm.1, bf16[256,2048]{1,0:T(8,128)(2,1)} %v_hbm.1, f32[3,3,2048]{2,1,0:T(4,128)} %sw_hbm.1, f32[16,2048]{1,0:T(8,128)} %rate_hbm.1, f32[16,2048]{1,0:T(8,128)} %res_hbm.1, f32[1,2048]{1,0:T(1,128)} %bitcast.1), custom_call_target="tpu_custom_call" | custom-call | tf_op jit(solution)/shard_map/pallas_call | solution.py:366
  21.4 1.0 %copy.9 = bf16[256,2048]{1,0:T(8,128)(2,1)} copy(bf16[256,2048]{1,0:T(8,128)(2,1)S(1)} %shard_map.73) | data formatting | bytes 2097152

commit v3 on v2

--- a/solution.py
+++ b/solution.py
@@ -19,6 +19,14 @@
         half = x.shape[0] // 2
         x = x[:half] + x[half:]
     return x[0]
+
+
+def apart(a, b, count):
+    total, place = 0, 1
+    while place < count:
+        total = total + place * lax.rem(lax.div(a, place) + lax.div(b, place), 2)
+        place *= 2
+    return total
 
 
 def layer_kernel(
@@ -190,7 +198,7 @@
     )
 
     def send_all(i, carry):
-        send_ends(lax.rem(me + i, parts)).start()
+        send_ends(apart(me, parts - i, parts)).start()
         return carry
 
     lax.fori_loop(1, parts, send_all, 0)
@@ -308,7 +316,8 @@
 
     lax.fori_loop(0, groups, repair, 0)
 
-    def finish(cg, carry):
+    def finish(i, carry):
+        cg = apart(me * own // (modes // SUBS), i, groups)
         lanes = lanes_of(cg)
         for p in range(per_group):
             owner = cg * per_group + p

time: 22.5 us -> 23.5 us (1.044)
  the two profiles are of different devices: /device:TPU:25 before, /device:TPU:0 now
where the time goes in v3:
time: 23.5 us; the launch traced here: 23.3 us
  Pallas kernels  22.3 us (95%)
  local copies, waits for them, and re-layouts  0.97 us (4%)
    pallas_call x1, Pallas kernels, per_device(): pl.pallas_call(functools.partial(layer_kernel, parts), out_shape=pltpu.VM...  22.3 us
    unnamed x1, local copies, waits for them, and re-layouts  0.97 us

profile of v3, /device:TPU:0, one launch (start us, length us, event | category | flops | bytes accessed | tf_op | source)
XLA Modules:
  0.0 23.3 jit_solution(10967900374144480685)
XLA Ops:
  0.0 22.3 %shard_map.73 = bf16[256,2048]{1,0:T(8,128)(2,1)S(1)} custom-call(bf16[256,2048]{1,0:T(8,128)(2,1)} %q_hbm.1, bf16[256,2048]{1,0:T(8,128)(2,1)} %k_hbm.1, bf16[256,2048]{1,0:T(8,128)(2,1)} %v_hbm.1, f32[3,3,2048]{2,1,0:T(4,128)} %sw_hbm.1, f32[16,2048]{1,0:T(8,128)} %rate_hbm.1, f32[16,2048]{1,0:T(8,128)} %res_hbm.1, f32[1,2048]{1,0:T(1,128)} %bitcast.1), custom_call_target="tpu_custom_call" | custom-call | tf_op jit(solution)/shard_map/pallas_call | solution.py:375
  22.4 1.0 %copy.9 = bf16[256,2048]{1,0:T(8,128)(2,1)} copy(bf16[256,2048]{1,0:T(8,128)(2,1)S(1)} %shard_map.73) | data formatting | bytes 2097152
